TPU v7x, 32 devices: a whole 2x2x4 slice. The times are simulated.
32 devices in a mesh: grid: 2 (over x), row: 4 (over y, core), col: 4 (over z).
Axes of the slice: x: 2, y: 2, z: 4, core: 2. Of those that a mesh axis runs over, the one named last changes fastest.
Arguments:
- rhs_in: bfloat16 [32768, 1024], P(('grid', 'row', 'col')), may hold values from -6 to 6
- rhs_target: int32 [32768], P(('grid', 'row', 'col')), may hold values from 0 to 32767, as said below
- leaf_inverse: bfloat16 [64, 512, 512], P(('grid', 'row', 'col')), may hold values from -0.25 to 0.25
- level_one_blocks: bfloat16 [2, 4, 4, 4, 2, 512, 512], P('grid', 'row', 'col'), may hold values from -0.0625 to 0.0625
- level_one_pattern: int32 [2, 4, 4, 4, 2], P('grid', 'row', 'col'), may hold values 0 or 1
- level_one_rhs: bfloat16 [2, 4, 512, 1024], P('grid', 'row', None, 'col'), may hold values from -6 to 6
- level_one_inverse: bfloat16 [2, 4, 512, 512], P('grid', 'row'), may hold values from -0.25 to 0.25
- top_blocks: bfloat16 [2, 4, 4, 512, 512], P('grid', 'row'), may hold values from -0.09375 to 0.09375
- top_rhs: bfloat16 [4, 512, 1024], P(None, None, 'col'), may hold values from -6 to 6
- top_inverse: bfloat16 [4, 512, 512], replicated, may hold values from -0.25 to 0.25
- top_chain: bfloat16 [6, 512, 512], replicated, may hold values from -0.125 to 0.125
Outputs:
- leaf_solution: bfloat16 [32768, 1024], P(('grid', 'row', 'col'))
- level_one_solution: bfloat16 [2, 4, 512, 1024], P('grid', 'row', None, 'col')
- top_solution: bfloat16 [4, 512, 1024], P(None, None, 'col')
Inputs may be any that keep to these rules, and one draw needn't show every extreme that they name: rhs_target is a permutation; position p belongs to the device of flat index p // 1024 over grid, row, col (grid slowest); the 1024 arrival rows of every device go exactly 32 to each device.
All inputs are finite; a program needn't handle non-finite values. No bound on the sum of `level_one_pattern` on one device may be relied on, other than what follows from the above.
Results may differ from a plain program's by a relative error of at most 0.02.
Values may be sent and summed in bfloat16 or wider, within the bound.
A program may use at most 128 MiB of HBM per device.

v0:
```python
import functools

import jax
import jax.numpy as jnp
from jax import lax
from jax.experimental import pallas as pl
from jax.experimental.pallas import tpu as pltpu
from jax.sharding import PartitionSpec as P

MESH = pl.DeviceIdType.MESH
VMEM = pl.BlockSpec(memory_space=pltpu.VMEM)
ANY = pl.BlockSpec(memory_space=pl.ANY)


def greet(axes, sizes):
    barrier = pltpu.get_barrier_semaphore()
    total = 1
    for size in sizes:
        total *= size
    flat = 0
    for axis, size in zip(axes, sizes):
        flat = flat * size + lax.axis_index(axis)

    @pl.loop(1, total)
    def _(step):
        rest = lax.rem(flat + step, total)
        coords = {}
        for axis, size in reversed(list(zip(axes, sizes))):
            coords[axis] = lax.rem(rest, size)
            rest = rest // size
        pl.semaphore_signal(barrier, inc=1, device_id=coords, device_id_type=MESH)

    return lambda: pl.semaphore_wait(barrier, total - 1)


def dot(a, b):
    return jnp.dot(a, b, preferred_element_type=jnp.float32)


def dot_t(a, b):
    return lax.dot_general(a, b, (((1,), (1,)), ((), ())), preferred_element_type=jnp.float32)


def lower_kernel(
    sizes,
    order,
    rhs_ref,
    slot_ref,
    place_ref,
    inverse_ref,
    blocks_hbm,
    pattern_ref,
    rhs_one_ref,
    inverse_one_ref,
    top_blocks_hbm,
    top_rhs_hbm,
    top_inverse_hbm,
    chain_hbm,
    leaf_ref,
    one_ref,
    top_ref,
    perm,
    fold,
    sorted_rows,
    got,
    got_places,
    own_blocks,
    other_blocks,
    other_pattern,
    solved,
    gathered,
    totals,
    pieces,
    landed,
    top_blocks,
    top_rhs,
    top_inverse,
    chain,
    rhs_turned,
    terms,
    mate_terms,
    summed,
    sums,
    load_sems,
    top_load_sems,
    block_sems,
    pattern_sems,
    place_send,
    place_recv,
    row_send,
    row_recv,
    gather_send,
    gather_recv,
    piece_send,
    piece_recv,
    mate_send,
    mate_recv,
    sum_send,
    sum_recv,
    out_send,
    out_recv,
    on_send,
    on_recv,
):
    grids, rows, cols = sizes
    devices = grids * rows * cols
    row = lax.axis_index("row")
    col = lax.axis_index("col")
    me = (lax.axis_index("grid") * rows + row) * cols + col
    side = lax.rem(row, 2)
    mate = row + 1 - 2 * side
    leaves, size, _ = inverse_ref.shape
    height = leaves * size
    chunk = leaf_ref.shape[1] // cols
    half = chunk // 2
    share = got.shape[2]
    group = 128 // share

    def row_at(offset):
        pair = lax.rem(row // 2 + offset // 2, rows // 2)
        return pair * 2 + lax.rem(side + offset % 2, 2)

    def device_of(flat):
        return {
            "grid": flat // (rows * cols),
            "row": lax.rem(flat // cols, rows),
            "col": lax.rem(flat, cols),
        }

    loads = [
        pltpu.make_async_copy(blocks_hbm.at[owner], own_blocks.at[owner], load_sems.at[owner])
        for owner in range(rows)
    ]
    met = greet(("grid", "row", "col"), sizes)
    for load in loads:
        load.start()
    top_loads = [
        pltpu.make_async_copy(source, into, top_load_sems.at[at])
        for at, (source, into) in enumerate(
            (
                (top_rhs_hbm, top_rhs),
                (top_blocks_hbm, top_blocks),
                (top_inverse_hbm, top_inverse),
                (chain_hbm, chain),
            )
        )
    ]
    for load in top_loads:
        load.start()

    def peer(step):
        return lax.rem(me + step, devices)

    def place_copy(step, slot):
        target = peer(step)
        return pltpu.make_async_remote_copy(
            src_ref=place_ref.at[target],
            dst_ref=got_places.at[slot],
            send_sem=place_send.at[target],
            recv_sem=place_recv.at[slot],
            device_id=device_of(target),
            device_id_type=MESH,
        )

    def row_copy(part, step, slot):
        target = peer(step)
        return pltpu.make_async_remote_copy(
            src_ref=sorted_rows.at[part, target],
            dst_ref=got.at[part, slot],
            send_sem=row_send.at[part, target],
            recv_sem=row_recv.at[part, slot],
            device_id=device_of(target),
            device_id_type=MESH,
        )

    def block_copy(owner):
        return pltpu.make_async_remote_copy(
            src_ref=blocks_hbm.at[owner],
            dst_ref=other_blocks.at[owner],
            send_sem=block_sems.at[0, owner],
            recv_sem=block_sems.at[1, owner],
            device_id={"row": mate},
            device_id_type=MESH,
        )

    def gather_copy(part, target, owner):
        return pltpu.make_async_remote_copy(
            src_ref=solved.at[part, lax.rem(target, 2)],
            dst_ref=gathered.at[part, owner],
            send_sem=gather_send.at[part, target],
            recv_sem=gather_recv.at[part, owner],
            device_id={"row": target},
            device_id_type=MESH,
        )

    def piece_copy(part, which, source, from_side):
        return pltpu.make_async_remote_copy(
            src_ref=pieces.at[part, which],
            dst_ref=landed.at[source, from_side],
            send_sem=piece_send.at[part, which],
            recv_sem=piece_recv.at[source, from_side],
            device_id={"row": mate if which else row, "col": part},
            device_id_type=MESH,
        )

    pattern_copy = pltpu.make_async_remote_copy(
        src_ref=pattern_ref,
        dst_ref=other_pattern,
        send_sem=pattern_sems.at[0],
        recv_sem=pattern_sems.at[1],
        device_id={"row": mate},
        device_id_type=MESH,
    )

    step_rows = 256
    for begin in range(0, height, step_rows):
        index = lax.broadcasted_iota(jnp.int32, (step_rows, height), 0) + begin
        perm[begin : begin + step_rows, :] = (
            jnp.where(index == slot_ref[...], 1.0, 0.0).astype(perm.dtype)
        )

    def send_rows(part):
        @pl.loop(1, devices)
        def _(step):
            row_copy(part, step, me).start()

    for at, part in enumerate(order):
        moved = dot(perm[...], rhs_ref[:, part * chunk : (part + 1) * chunk]).astype(got.dtype)
        sorted_rows[part] = moved.reshape(devices, share, chunk)
        if at == 0:
            met()

            @pl.loop(1, devices)
            def _(step):
                place_copy(step, me).start()

        if at < 2:
            send_rows(part)
        got[part, me] = sorted_rows[part, me]
    pattern_copy.start()
    for owner in range(rows):
        block_copy(owner).start()

    got_places[me] = place_ref[me]

    @pl.loop(1, devices)
    def _(step):
        place_copy(step, peer(step)).wait_recv()

    for block in range(height // 128):
        places = got_places[block * group]
        for other in range(1, group):
            places = places + got_places[block * group + other]
        index = lax.broadcasted_iota(jnp.int32, (height, 128), 0)
        perm[:, block * 128 : (block + 1) * 128] = jnp.where(index == places, 1.0, 0.0).astype(
            perm.dtype
        )
    for leaf in range(leaves):
        span = slice(leaf * size, (leaf + 1) * size)
        fold[span, :] = dot(inverse_ref[leaf], perm[span, :]).astype(fold.dtype)

    def masked(block, mask):
        tall = block.shape[0] // mask.shape[0]
        return (block.reshape(tall, *mask.shape) * mask[None]).reshape(block.shape)

    for load in loads + top_loads:
        load.wait()

    tops = top_blocks.shape[0]
    pairs = grids * rows // 2
    depth = terms.shape[3]
    for top in range(tops):
        rhs_turned[top] = top_rhs[top].T.reshape(2 * pairs, depth, size)

    @pl.loop(0, rows)
    def _(owner):
        for leaf in range(leaves):
            own_blocks[owner, leaf] = masked(own_blocks[owner, leaf], pattern_ref[owner, leaf])

    def solve(part):
        @pl.loop(1, devices)
        def _(step):
            row_copy(part, step, peer(step)).wait_recv()

        result = dot(fold[...], got[part].reshape(height, chunk)).astype(leaf_ref.dtype)
        leaf_ref[:, part * chunk : (part + 1) * chunk] = result
        for which in range(2):
            solved[part, which] = result[:, which * half : (which + 1) * half]
        for offset in range(rows - 1, 0, -1):
            gather_copy(part, row_at(offset), row).start()
        gathered[part, row] = solved[part, side]

    def add(part, owner):
        for which, blocks in enumerate((own_blocks, other_blocks)):
            term = dot(blocks[owner, 0], gathered[part, owner, :size])
            for leaf in range(1, leaves):
                term = term + dot(
                    blocks[owner, leaf], gathered[part, owner, leaf * size : (leaf + 1) * size]
                )
            totals[which] += term

    def couple(part):
        totals[...] = jnp.zeros_like(totals)

        @pl.loop(0, rows)
        def _(offset):
            owner = row_at(offset)

            @pl.when(offset > 0)
            def _():
                gather_copy(part, owner, owner).wait_recv()

            add(part, owner)

        pieces[part] = totals[...].astype(pieces.dtype)
        piece_copy(part, 1, col, side).start()

        @pl.when(col != part)
        def _():
            piece_copy(part, 0, col, side).start()

        @pl.when(col == part)
        def _():
            landed[col, side] = pieces[part, 0]

    for at, part in enumerate(order):
        solve(part)
        if at + 2 < cols:
            send_rows(order[at + 2])
        if at == 0:
            pattern_copy.wait()

            @pl.loop(0, rows)
            def _(owner):
                block_copy(owner).wait()
                for leaf in range(leaves):
                    other_blocks[owner, leaf] = masked(
                        other_blocks[owner, leaf], other_pattern[owner, leaf]
                    )
        else:
            couple(order[at - 1])
    couple(order[-1])

    for step in range(cols):
        source = lax.rem(col + step, cols)
        piece_copy(0, 1, source, 1 - side).wait_recv()
        if step:
            piece_copy(0, 0, source, side).wait_recv()
    update = []
    for which in range(2):
        total = landed[0, which].astype(jnp.float32)
        for source in range(1, cols):
            total = total + landed[source, which].astype(jnp.float32)
        update.append(total)
    resid = rhs_one_ref[...].astype(jnp.float32) - jnp.concatenate(update, axis=1)
    solution_one = dot(inverse_one_ref[...], resid.astype(jnp.bfloat16)).astype(one_ref.dtype)
    one_ref[...] = solution_one

    pair = (lax.axis_index("grid") * rows + row) // 2
    here = 2 * pair + side

    def pair_at(step):
        return lax.rem(pair + step, pairs)

    def across(target):
        return {
            "grid": target // (rows // 2),
            "row": lax.rem(target, rows // 2) * 2 + side,
        }

    def mate_copy(top):
        return pltpu.make_async_remote_copy(
            src_ref=terms.at[top, 1 - side],
            dst_ref=mate_terms.at[top],
            send_sem=mate_send.at[top],
            recv_sem=mate_recv.at[top],
            device_id={"row": mate},
            device_id_type=MESH,
        )

    def sum_copy(top, target, source):
        return pltpu.make_async_remote_copy(
            src_ref=summed.at[top, target],
            dst_ref=sums.at[top, source],
            send_sem=sum_send.at[top, target],
            recv_sem=sum_recv.at[top, source],
            device_id=across(target),
            device_id_type=MESH,
        )

    def out_copy(top, target, source):
        return pltpu.make_async_remote_copy(
            src_ref=top_ref.at[here, top],
            dst_ref=top_ref.at[2 * source + side, top],
            send_sem=out_send.at[top, target],
            recv_sem=out_recv.at[top, source],
            device_id=across(target),
            device_id_type=MESH,
        )

    def on_copy(top, source, from_side):
        return pltpu.make_async_remote_copy(
            src_ref=top_ref.at[2 * source + side, top],
            dst_ref=top_ref.at[2 * source + from_side, top],
            send_sem=on_send.at[top, source],
            recv_sem=on_recv.at[top, source],
            device_id={"row": mate},
            device_id_type=MESH,
        )

    turned = solution_one.T
    for top in range(tops):
        term = dot_t(turned, top_blocks[top])
        for target in range(2 * pairs):
            terms[top, target % 2, target // 2] = term[
                target * depth : (target + 1) * depth
            ].astype(terms.dtype)
        mate_copy(top).start()
    for top in range(tops):
        mate_copy(top).wait_recv()
        summed[top] = (
            terms[top, side].astype(jnp.float32) + mate_terms[top].astype(jnp.float32)
        ).astype(summed.dtype)
        for step in range(1, pairs):
            sum_copy(top, pair_at(step), pair).start()
    for top in range(tops):
        sums[top, pair] = summed[top, pair]
        for step in range(1, pairs):
            sum_copy(top, pair_at(step), pair_at(step)).wait_recv()
        update = sums[top, 0].astype(jnp.float32)
        for other in range(1, pairs):
            update = update + sums[top, other].astype(jnp.float32)
        running = rhs_turned[top, here].astype(jnp.float32) - update
        for earlier in range(top):
            running = running - dot_t(
                top_ref[here, earlier], chain[top * (top - 1) // 2 + earlier]
            )
        top_ref[here, top] = dot_t(running.astype(jnp.bfloat16), top_inverse[top]).astype(
            top_ref.dtype
        )
        for step in range(1, pairs):
            out_copy(top, pair_at(step), pair).start()
        on_copy(top, pair, side).start()
    for top in range(tops):
        for step in range(1, pairs):
            source = pair_at(step)
            out_copy(top, source, source).wait_recv()
            on_copy(top, source, side).start()
    for top in range(tops):
        for step in range(pairs):
            on_copy(top, pair_at(step), 1 - side).wait_recv()
        for step in range(pairs):
            on_copy(top, pair_at(step), side).wait_send()
            if step:
                out_copy(top, pair_at(step), pair).wait_send()
                sum_copy(top, pair_at(step), pair).wait_send()
        mate_copy(top).wait_send()

    for part in range(cols):
        piece_copy(part, 1, col, side).wait_send()

        @pl.when(col != part)
        def _(part=part):
            piece_copy(part, 0, col, side).wait_send()

        for offset in range(1, rows):
            gather_copy(part, row_at(offset), row).wait_send()

        @pl.loop(1, devices)
        def _(step, part=part):
            row_copy(part, step, me).wait_send()

    @pl.loop(1, devices)
    def _(step):
        place_copy(step, me).wait_send()


def all_levels(rhs_in, target, leaf_inverse, blocks, pattern, rhs, inverse, *top_arrays):
    sizes = tuple(lax.axis_size(axis) for axis in ("grid", "row", "col"))
    grids, rows, cols = sizes
    devices = grids * rows * cols
    height, width = rhs_in.shape
    share = height // devices
    owners, leaves, size, _ = blocks.shape
    chunk = width // cols
    half = chunk // 2
    bf16 = jnp.bfloat16
    order = sorted(range(cols), key=lambda part: -abs(2 * part - (cols - 1)))

    destination = target // height
    place = target % height
    index = jnp.arange(height, dtype=jnp.int32)
    same = (destination[:, None] == destination[None, :]) & (index[:, None] < index[None, :])
    slot = destination * share + jnp.sum(same.astype(jnp.int32), axis=0)
    picked = jnp.where(slot[None, :] == index[:, None], place[None, :], 0)
    sorted_places = jnp.sum(picked, axis=1).reshape(devices, 1, share)
    group = 128 // share
    me = lax.axis_index(("grid", "row", "col"))
    lane_group = jnp.arange(128, dtype=jnp.int32) // share
    place_rows = jnp.where(
        lane_group == me % group, jnp.tile(sorted_places, (1, 1, group)), 0
    )

    mask = jnp.broadcast_to(pattern.astype(bf16)[:, :, None, None], (owners, leaves, 16, size))
    dma = pltpu.SemaphoreType.DMA
    tops, _, top_width = top_arrays[1].shape
    pairs = grids * rows // 2
    depth = top_width // (2 * pairs)
    leaf, one, stacked = pl.pallas_call(
        functools.partial(lower_kernel, sizes, order),
        out_shape=(
            jax.ShapeDtypeStruct((height, width), bf16),
            jax.ShapeDtypeStruct(rhs.shape, bf16),
            jax.ShapeDtypeStruct((2 * pairs, tops, depth, size), bf16),
        ),
        in_specs=[VMEM, VMEM, VMEM, VMEM, ANY, VMEM, VMEM, VMEM, ANY, ANY, ANY, ANY],
        out_specs=(VMEM, VMEM, VMEM),
        scratch_shapes=[
            pltpu.VMEM((height, height), bf16),
            pltpu.VMEM((height, height), bf16),
            pltpu.VMEM((cols, devices, share, chunk), bf16),
            pltpu.VMEM((cols, devices, share, chunk), bf16),
            pltpu.VMEM((devices, 1, 128), jnp.int32),
            pltpu.VMEM(blocks.shape, bf16),
            pltpu.VMEM(blocks.shape, bf16),
            pltpu.VMEM(mask.shape, bf16),
            pltpu.VMEM((cols, 2, height, half), bf16),
            pltpu.VMEM((cols, rows, height, half), bf16),
            pltpu.VMEM((2, size, half), jnp.float32),
            pltpu.VMEM((cols, 2, size, half), bf16),
            pltpu.VMEM((cols, 2, size, half), bf16),
            *(pltpu.VMEM(array.shape, bf16) for array in top_arrays),
            pltpu.VMEM((tops, 2 * pairs, depth, size), bf16),
            pltpu.VMEM((tops, 2, pairs, depth, size), bf16),
            pltpu.VMEM((tops, pairs, depth, size), bf16),
            pltpu.VMEM((tops, pairs, depth, size), bf16),
            pltpu.VMEM((tops, pairs, depth, size), bf16),
            dma((rows,)),
            dma((len(top_arrays),)),
            dma((2, rows)),
            dma((2,)),
            dma((devices,)),
            dma((devices,)),
            dma((cols, devices)),
            dma((cols, devices)),
            dma((cols, rows)),
            dma((cols, rows)),
            dma((cols, 2)),
            dma((cols, 2)),
            dma((tops,)),
            dma((tops,)),
            *(dma((tops, pairs)) for _ in range(6)),
        ],
        compiler_params=pltpu.CompilerParams(
            collective_id=1, has_side_effects=True, vmem_limit_bytes=60 * 2**20
        ),
        name="lower",
    )(rhs_in, slot[None, :], place_rows, leaf_inverse, blocks, mask, rhs, inverse, *top_arrays)
    solved = jnp.transpose(stacked, (1, 3, 0, 2)).reshape(tops, size, top_width)
    return leaf, one, solved


def shards(
    rhs_in,
    rhs_target,
    leaf_inverse,
    level_one_blocks,
    level_one_pattern,
    level_one_rhs,
    level_one_inverse,
    top_blocks,
    top_rhs,
    top_inverse,
    top_chain,
):
    leaf_solution, solution_one, top_solution = all_levels(
        rhs_in,
        rhs_target,
        leaf_inverse,
        level_one_blocks[0, 0, 0],
        level_one_pattern[0, 0, 0],
        level_one_rhs[0, 0],
        level_one_inverse[0, 0],
        top_blocks[0, 0],
        top_rhs,
        top_inverse,
        top_chain,
    )
    return (leaf_solution, solution_one[None, None], top_solution)


def solution(mesh):
    in_specs = (
        P(("grid", "row", "col"), None),
        P(("grid", "row", "col")),
        P(("grid", "row", "col"), None, None),
        P("grid", "row", "col", None, None, None, None),
        P("grid", "row", "col", None, None),
        P("grid", "row", None, "col"),
        P("grid", "row", None, None),
        P("grid", "row", None, None, None),
        P(None, None, "col"),
        P(),
        P(),
    )
    out_specs = (
        P(("grid", "row", "col"), None),
        P("grid", "row", None, "col"),
        P(None, None, "col"),
    )
    return jax.shard_map(shards, mesh=mesh, in_specs=in_specs, out_specs=out_specs, check_vma=False)
```

profile of v0, /device:TPU:17, one launch (start us, length us, event | category | flops | bytes accessed | tf_op | source)
XLA Modules:
  0.0 134.2 jit_solution(11671023165446874445)
XLA Ops:
  0.7 0.7 convert_bitcast_fusion
  1.3 0.1 copy.18
  1.5 0.7 add_select_fusion.1
  2.1 0.4 convert_reduce_fusion
  2.6 0.7 add_select_fusion
  3.3 0.0 copy-start.2
  3.3 0.5 select_reduce_fusion
  3.8 0.1 tile.10
  3.9 0.1 tile.12
  4.0 0.6 broadcast_select_fusion.place_ref
  4.6 0.7 broadcast_in_dim.44.pattern_ref
  5.3 0.0 copy-done.2
  5.3 124.1 %lower.1 = (bf16[1024,1024]{1,0:T(8,128)(2,1)}, bf16[512,256]{1,0:T(8,128)(2,1)}, bf16[8,4,32,512]{3,2,1,0:T(8,128)(2,1)}) custom-call(bf16[1024,1024]{1,0:T(8,128)(2,1)} %rhs_ref.1, s32[1,1024]{1,0:T(1,128)} %bitcast.17, s32[32,1,128]{2,1,0:T(1,128)} %broadcast_select_fusion.place_ref, bf16[2,512,512]{2,1,0:T(8,128)(2,1)} %inverse_ref.1, ...), custom_call_target="tpu_custom_call" | custom-call | tf_op jit(solution)/shard_map/lower/pallas_call | solution.py:509
  129.4 0.0 copy-start
  129.4 0.0 copy-start.1
  129.4 1.4 %copy.19 = bf16[4,512,8,32]{1,3,2,0:T(8,128)(2,1)S(1)} copy(bf16[4,512,8,32]{1,3,0,2:T(8,128)(2,1)} %bitcast.13) | data formatting | bytes 2097152 | tf_op jit(solution)/shard_map/transpose | solution.py:559
  130.9 1.3 copy.20
  132.2 0.0 copy-done
  132.2 1.3 copy.23
  133.5 0.0 copy-done.1
  133.5 0.7 copy.24
  (2 shorter events, 0.0 us)
Async XLA Ops:
  3.3 2.1 %copy-start.2 = (s32[1024]{0:T(1024)}, s32[1024]{0:T(1024)S(1)}, u32[]{:S(2)}) copy-start(s32[1024]{0:T(1024)S(1)} %get-tuple-element.16) | copy-start | bytes 12292
  129.4 2.8 %copy-start = (bf16[1024,1024]{1,0:T(8,128)(2,1)S(1)}, bf16[1024,1024]{1,0:T(8,128)(2,1)}, u32[]{:S(2)}) copy-start(bf16[1024,1024]{1,0:T(8,128)(2,1)} %get-tuple-element.20) | copy-start | bytes 6291460
  129.4 4.1 %copy-start.1 = (bf16[512,256]{1,0:T(8,128)(2,1)S(1)}, bf16[512,256]{1,0:T(8,128)(2,1)}, u32[]{:S(2)}) copy-start(bf16[512,256]{1,0:T(8,128)(2,1)} %get-tuple-element.7) | copy-start | bytes 786436
where the time goes:
time: 134 us
  Pallas kernels  124 us (93%)
  local copies, waits for them, and re-layouts  5.83 us (4%)
  other arithmetic  3.62 us (3%)
    pallas_call x1, Pallas kernels, all_levels(): pl.pallas_call(functools.partial(lower_kernel, sizes, order), out_shape=(...  124 us
    unnamed x9, local copies, waits for them, and re-layouts  3.34 us

commit v1 on v0

v1 whole, which is shorter than its diff:
```python
import functools

import jax
import jax.numpy as jnp
from jax import lax
from jax.experimental import pallas as pl
from jax.experimental.pallas import tpu as pltpu
from jax.sharding import PartitionSpec as P

MESH = pl.DeviceIdType.MESH
ANY = pl.BlockSpec(memory_space=pl.ANY)


def greet(axes, sizes):
    barrier = pltpu.get_barrier_semaphore()
    total = 1
    for size in sizes:
        total *= size
    flat = 0
    for axis, size in zip(axes, sizes):
        flat = flat * size + lax.axis_index(axis)

    @pl.loop(1, total)
    def _(step):
        rest = lax.rem(flat + step, total)
        coords = {}
        for axis, size in reversed(list(zip(axes, sizes))):
            coords[axis] = lax.rem(rest, size)
            rest = rest // size
        pl.semaphore_signal(barrier, inc=1, device_id=coords, device_id_type=MESH)

    return lambda: pl.semaphore_wait(barrier, total - 1)


def dot(a, b):
    return jnp.dot(a, b, preferred_element_type=jnp.float32)


def dot_t(a, b):
    return lax.dot_general(a, b, (((1,), (1,)), ((), ())), preferred_element_type=jnp.float32)


def lower_kernel(
    sizes,
    order,
    target_hbm,
    rhs_hbm,
    inverse_hbm,
    blocks_hbm,
    pattern_ref,
    rhs_one_hbm,
    inverse_one_hbm,
    top_rhs_hbm,
    top_blocks_hbm,
    top_inverse_hbm,
    chain_hbm,
    leaf_hbm,
    one_hbm,
    top_hbm,
    targets,
    rhs,
    inverse,
    own_blocks,
    rhs_one,
    inverse_one,
    top_rhs,
    top_blocks,
    top_inverse,
    chain,
    perm,
    fold,
    sorted_rows,
    got,
    places_out,
    got_places,
    other_blocks,
    solved,
    gathered,
    totals,
    pieces,
    landed,
    rhs_turned,
    terms,
    mate_terms,
    summed,
    sums,
    stacked,
    leaf,
    one,
    top_out,
    load_sems,
    leaf_sems,
    result_sems,
    block_sems,
    place_sems,
    row_send,
    row_recv,
    gather_send,
    gather_recv,
    piece_send,
    piece_recv,
    mate_send,
    mate_recv,
    sum_send,
    sum_recv,
    out_send,
    out_recv,
    on_send,
    on_recv,
):
    grids, rows, cols = sizes
    devices = grids * rows * cols
    row = lax.axis_index("row")
    col = lax.axis_index("col")
    me = (lax.axis_index("grid") * rows + row) * cols + col
    side = lax.rem(row, 2)
    mate = row + 1 - 2 * side
    leaves, size, _ = inverse.shape
    height = leaves * size
    chunk = leaf.shape[1] // cols
    half = chunk // 2
    share = got.shape[2]
    group = 128 // share

    met = greet(("grid", "row", "col"), sizes)
    loads = [
        pltpu.make_async_copy(source, into, load_sems.at[at])
        for at, (source, into) in enumerate(
            (
                (target_hbm, targets),
                (rhs_hbm, rhs),
                (inverse_hbm, inverse),
                (blocks_hbm, own_blocks),
                (rhs_one_hbm, rhs_one),
                (inverse_one_hbm, inverse_one),
                (top_rhs_hbm, top_rhs),
                (top_blocks_hbm, top_blocks),
                (top_inverse_hbm, top_inverse),
                (chain_hbm, chain),
            )
        )
    ]
    for load in loads:
        load.start()

    def column_of(part, which):
        pair = order[part // 2 * 2 : part // 2 * 2 + 2]
        return pair[which] if part % 2 == 0 else pair[1 - which]

    def columns(part, which):
        begin = column_of(part, which) * chunk + part % 2 * half
        return slice(begin, begin + half)

    def row_at(offset):
        pair = lax.rem(row // 2 + offset // 2, rows // 2)
        return pair * 2 + lax.rem(side + offset % 2, 2)

    def device_of(flat):
        return {
            "grid": flat // (rows * cols),
            "row": lax.rem(flat // cols, rows),
            "col": lax.rem(flat, cols),
        }

    def drain(ref, sem):
        pltpu.make_async_copy(ref, ref, sem).wait()

    def peer(step):
        return lax.rem(me + step, devices)

    def place_copy(step):
        target = peer(step)
        return pltpu.make_async_remote_copy(
            src_ref=places_out.at[target],
            dst_ref=got_places.at[me],
            send_sem=place_sems.at[0],
            recv_sem=place_sems.at[1],
            device_id=device_of(target),
            device_id_type=MESH,
        )

    def row_copy(part, step):
        target = peer(step)
        return pltpu.make_async_remote_copy(
            src_ref=sorted_rows.at[part, target],
            dst_ref=got.at[part, me],
            send_sem=row_send.at[part],
            recv_sem=row_recv.at[part],
            device_id=device_of(target),
            device_id_type=MESH,
        )

    block_copy = pltpu.make_async_remote_copy(
        src_ref=own_blocks,
        dst_ref=other_blocks,
        send_sem=block_sems.at[0],
        recv_sem=block_sems.at[1],
        device_id={"row": mate},
        device_id_type=MESH,
    )

    def gather_copy(part, target, owner):
        return pltpu.make_async_remote_copy(
            src_ref=solved.at[part, lax.rem(target, 2)],
            dst_ref=gathered.at[part, owner],
            send_sem=gather_send.at[part],
            recv_sem=gather_recv.at[part, owner],
            device_id={"row": target},
            device_id_type=MESH,
        )

    def piece_copy(part, which, into):
        return pltpu.make_async_remote_copy(
            src_ref=pieces.at[part, which],
            dst_ref=landed.at[part % 2, col],
            send_sem=piece_send.at[which],
            recv_sem=piece_recv.at[part % 2],
            device_id={"row": mate if which else row, "col": into},
            device_id_type=MESH,
        )

    span = height
    before = lax.broadcasted_iota(jnp.int32, (span, span), 0)
    after = lax.broadcasted_iota(jnp.int32, (span, span), 1)
    perm[...] = jnp.where(before < after, 1.0, 0.0).astype(perm.dtype)
    loads[0].wait()
    destination = targets[...] // height
    place = lax.rem(targets[...], height)
    for_device = lax.broadcasted_iota(jnp.int32, (devices, height), 0) == destination
    ones = jnp.where(for_device, 1.0, 0.0)
    counted = dot(ones.astype(perm.dtype), perm[...])
    rank = jnp.sum(ones * counted, axis=0, keepdims=True).astype(jnp.int32)
    slot = destination * share + rank

    step_rows = 256
    for begin in range(0, height, step_rows):
        index = lax.broadcasted_iota(jnp.int32, (step_rows, height), 0) + begin
        perm[begin : begin + step_rows, :] = (
            jnp.where(index == slot, 1.0, 0.0).astype(perm.dtype)
        )
    loads[1].wait()

    def send_rows(part):
        @pl.loop(1, devices)
        def _(step):
            row_copy(part, step).start()

    for part in range(cols):
        taken = jnp.concatenate([rhs[:, columns(part, which)] for which in range(2)], axis=1)
        moved = dot(perm[...], taken).astype(got.dtype)
        sorted_rows[part] = moved.reshape(devices, share, chunk)
        if part == 0:
            met()
        if part < 2:
            send_rows(part)
        got[part, me] = sorted_rows[part, me]
        if part == 0:
            lane = lax.broadcasted_iota(jnp.int32, (128, height), 0)
            to_lane = jnp.where(lane == lax.rem(me, group) * share + rank, 1.0, 0.0)
            to_lane = to_lane.astype(perm.dtype)
            high = (ones * (place // 32).astype(jnp.float32)).astype(perm.dtype)
            low = (ones * lax.rem(place, 32).astype(jnp.float32)).astype(perm.dtype)
            spread = dot_t(high, to_lane) * 32.0 + dot_t(low, to_lane)
            places_out[...] = spread.astype(jnp.int32).reshape(devices, 1, 128)

            @pl.loop(1, devices)
            def _(step):
                place_copy(step).start()

            got_places[me] = places_out[me]

    def masked(block, scale):
        return (block.astype(jnp.float32) * scale).astype(block.dtype)

    loads[3].wait()

    @pl.loop(0, rows)
    def _(owner):
        for leaf_at in range(leaves):
            own_blocks[owner, leaf_at] = masked(
                own_blocks[owner, leaf_at], pattern_ref[owner, leaf_at].astype(jnp.float32)
            )

    block_copy.start()
    loads[2].wait()
    drain(got_places.at[pl.ds(0, devices - 1)], place_sems.at[1])

    for block in range(height // 128):
        places = got_places[block * group]
        for other in range(1, group):
            places = places + got_places[block * group + other]
        index = lax.broadcasted_iota(jnp.int32, (height, 128), 0)
        perm[:, block * 128 : (block + 1) * 128] = jnp.where(index == places, 1.0, 0.0).astype(
            perm.dtype
        )
    for at in range(leaves):
        of_leaf = slice(at * size, (at + 1) * size)
        fold[of_leaf, :] = dot(inverse[at], perm[of_leaf, :]).astype(fold.dtype)

    for load in loads[4:]:
        load.wait()

    tops = top_blocks.shape[0]
    pairs = grids * rows // 2
    depth = terms.shape[3]
    for top in range(tops):
        rhs_turned[top] = top_rhs[top].T.reshape(2 * pairs, depth, size)

    def leaf_copy(part, which):
        return pltpu.make_async_copy(
            leaf.at[:, columns(part, which)], leaf_hbm.at[:, columns(part, which)], leaf_sems.at[part, which]
        )

    def solve(part):
        drain(got.at[part, pl.ds(0, devices - 1)], row_recv.at[part])
        result = dot(fold[...], got[part].reshape(height, chunk)).astype(leaf.dtype)
        for which in range(2):
            solved[part, which] = result[:, which * half : (which + 1) * half]
        for offset in range(rows - 1, 0, -1):
            gather_copy(part, row_at(offset), row).start()
        gathered[part, row] = solved[part, side]
        for which in range(2):
            leaf[:, columns(part, which)] = result[:, which * half : (which + 1) * half]
            leaf_copy(part, which).start()

    def add(part, owner):
        for which, blocks in enumerate((own_blocks, other_blocks)):
            term = dot(blocks[owner, 0], gathered[part, owner, :size])
            for at in range(1, leaves):
                term = term + dot(
                    blocks[owner, at], gathered[part, owner, at * size : (at + 1) * size]
                )
            totals[which] += term

    def couple(part):
        totals[...] = jnp.zeros_like(totals)

        @pl.loop(0, rows)
        def _(offset):
            owner = row_at(offset)

            @pl.when(offset > 0)
            def _():
                gather_copy(part, owner, owner).wait_recv()

            add(part, owner)

        into = column_of(part, 0) + side * (column_of(part, 1) - column_of(part, 0))
        pieces[part] = totals[...].astype(pieces.dtype)
        piece_copy(part, 1, into).start()

        @pl.when(col != into)
        def _():
            piece_copy(part, 0, into).start()

        @pl.when(col == into)
        def _():
            landed[part % 2, col] = pieces[part, 0]

    for part in range(cols):
        solve(part)
        if part + 2 < cols:
            send_rows(part + 2)
        if part == 0:
            block_copy.wait()
        else:
            couple(part - 1)
    couple(cols - 1)

    second = 0
    for at in range(1, cols, 2):
        second = second + jnp.where(col == order[at], 1, 0)
    near = side + second - 2 * side * second
    drain(landed.at[near, pl.ds(0, cols - 1)], piece_recv.at[near])
    drain(landed.at[1 - near], piece_recv.at[1 - near])
    update = []
    for which in range(2):
        total = landed[which, 0].astype(jnp.float32)
        for source in range(1, cols):
            total = total + landed[which, source].astype(jnp.float32)
        update.append(total)
    resid = rhs_one[...].astype(jnp.float32) - jnp.concatenate(update, axis=1)
    solution_one = dot(inverse_one[...], resid.astype(jnp.bfloat16)).astype(one.dtype)

    pair = (lax.axis_index("grid") * rows + row) // 2
    here = 2 * pair + side

    def pair_at(step):
        return lax.rem(pair + step, pairs)

    def across(target):
        return {
            "grid": target // (rows // 2),
            "row": lax.rem(target, rows // 2) * 2 + side,
        }

    def mate_copy(top):
        return pltpu.make_async_remote_copy(
            src_ref=terms.at[top, 1 - side],
            dst_ref=mate_terms.at[top],
            send_sem=mate_send.at[top],
            recv_sem=mate_recv.at[top],
            device_id={"row": mate},
            device_id_type=MESH,
        )

    def sum_copy(top, target):
        return pltpu.make_async_remote_copy(
            src_ref=summed.at[top, target],
            dst_ref=sums.at[top, pair],
            send_sem=sum_send,
            recv_sem=sum_recv.at[top],
            device_id=across(target),
            device_id_type=MESH,
        )

    def out_copy(top, target, source):
        return pltpu.make_async_remote_copy(
            src_ref=stacked.at[top, here],
            dst_ref=stacked.at[top, 2 * source + side],
            send_sem=out_send,
            recv_sem=out_recv.at[top, source],
            device_id=across(target),
            device_id_type=MESH,
        )

    def on_copy(top, source):
        return pltpu.make_async_remote_copy(
            src_ref=stacked.at[top, 2 * source + side],
            dst_ref=stacked.at[top, 2 * source + side],
            send_sem=on_send,
            recv_sem=on_recv.at[top],
            device_id={"row": mate},
            device_id_type=MESH,
        )

    turned = solution_one.T
    for top in range(tops):
        term = dot_t(turned, top_blocks[top])
        for target in range(2 * pairs):
            terms[top, target % 2, target // 2] = term[
                target * depth : (target + 1) * depth
            ].astype(terms.dtype)
        mate_copy(top).start()
    one[...] = solution_one
    one_copy = pltpu.make_async_copy(one, one_hbm, result_sems.at[tops])
    one_copy.start()
    for top in range(tops):
        mate_copy(top).wait_recv()
        summed[top] = (
            terms[top, side].astype(jnp.float32) + mate_terms[top].astype(jnp.float32)
        ).astype(summed.dtype)
        for step in range(1, pairs):
            sum_copy(top, pair_at(step)).start()
    for top in range(tops):
        sums[top, pair] = summed[top, pair]
        drain(sums.at[top, pl.ds(0, pairs - 1)], sum_recv.at[top])
        update = sums[top, 0].astype(jnp.float32)
        for other in range(1, pairs):
            update = update + sums[top, other].astype(jnp.float32)
        running = rhs_turned[top, here].astype(jnp.float32) - update
        for earlier in range(top):
            running = running - dot_t(
                stacked[earlier, here], chain[top * (top - 1) // 2 + earlier]
            )
        stacked[top, here] = dot_t(running.astype(jnp.bfloat16), top_inverse[top]).astype(
            stacked.dtype
        )
        for step in range(1, pairs):
            out_copy(top, pair_at(step), pair).start()
        on_copy(top, pair).start()
    top_copies = [
        pltpu.make_async_copy(top_out.at[top], top_hbm.at[top], result_sems.at[top])
        for top in range(tops)
    ]
    for top in range(tops):
        for step in range(1, pairs):
            source = pair_at(step)
            out_copy(top, source, source).wait_recv()
            on_copy(top, source).start()
        drain(stacked.at[top, pl.ds(0, pairs)], on_recv.at[top])
        top_out[top] = stacked[top].reshape(2 * pairs * depth, size).T
        top_copies[top].start()

    drain(places_out.at[pl.ds(0, devices - 1)], place_sems.at[0])
    drain(pieces.at[:, 1], piece_send.at[1])

    for part in range(cols):
        drain(sorted_rows.at[part, pl.ds(0, devices - 1)], row_send.at[part])
        drain(gathered.at[part, pl.ds(0, rows - 1)], gather_send.at[part])
        for which in range(2):
            leaf_copy(part, which).wait()
    drain(pieces.at[pl.ds(0, cols - 1), 0], piece_send.at[0])
    for top in range(tops):
        mate_copy(top).wait_send()
        top_copies[top].wait()
    drain(summed.at[:, pl.ds(0, pairs - 1)], sum_send)
    drain(stacked.at[:, pl.ds(0, pairs - 1)], out_send)
    drain(stacked.at[:, pl.ds(0, pairs)], on_send)
    one_copy.wait()


def all_levels(rhs_in, target, leaf_inverse, blocks, pattern, rhs, inverse, top_blocks, top_rhs, *rest):
    sizes = tuple(lax.axis_size(axis) for axis in ("grid", "row", "col"))
    grids, rows, cols = sizes
    devices = grids * rows * cols
    height, width = rhs_in.shape
    share = height // devices
    owners, leaves, size, _ = blocks.shape
    chunk = width // cols
    half = chunk // 2
    bf16 = jnp.bfloat16
    order = sorted(range(cols), key=lambda part: -abs(2 * part - (cols - 1)))

    dma = pltpu.SemaphoreType.DMA
    tops = top_blocks.shape[0]
    pairs = grids * rows // 2
    depth = chunk // (2 * pairs)
    held = (rhs_in, leaf_inverse, blocks, rhs, inverse, top_rhs, top_blocks, *rest)
    smem = pl.BlockSpec(memory_space=pltpu.SMEM)
    return pl.pallas_call(
        functools.partial(lower_kernel, sizes, order),
        out_shape=(
            jax.ShapeDtypeStruct((height, width), bf16),
            jax.ShapeDtypeStruct(rhs.shape, bf16),
            jax.ShapeDtypeStruct(top_rhs.shape, bf16),
        ),
        in_specs=[ANY, ANY, ANY, ANY, smem, *(ANY for _ in range(6))],
        out_specs=(ANY, ANY, ANY),
        scratch_shapes=[
            pltpu.VMEM((1, height), jnp.int32),
            *(pltpu.VMEM(array.shape, bf16) for array in held),
            pltpu.VMEM((height, height), bf16),
            pltpu.VMEM((height, height), bf16),
            pltpu.VMEM((cols, devices, share, chunk), bf16),
            pltpu.VMEM((cols, devices, share, chunk), bf16),
            pltpu.VMEM((devices, 1, 128), jnp.int32),
            pltpu.VMEM((devices, 1, 128), jnp.int32),
            pltpu.VMEM(blocks.shape, bf16),
            pltpu.VMEM((cols, 2, height, half), bf16),
            pltpu.VMEM((cols, rows, height, half), bf16),
            pltpu.VMEM((2, size, half), jnp.float32),
            pltpu.VMEM((cols, 2, size, half), bf16),
            pltpu.VMEM((2, cols, size, half), bf16),
            pltpu.VMEM((tops, 2 * pairs, depth, size), bf16),
            pltpu.VMEM((tops, 2, pairs, depth, size), bf16),
            pltpu.VMEM((tops, pairs, depth, size), bf16),
            pltpu.VMEM((tops, pairs, depth, size), bf16),
            pltpu.VMEM((tops, pairs, depth, size), bf16),
            pltpu.VMEM((tops, 2 * pairs, depth, size), bf16),
            pltpu.VMEM((height, width), bf16),
            pltpu.VMEM(rhs.shape, bf16),
            pltpu.VMEM(top_rhs.shape, bf16),
            dma((len(held) + 1,)),
            dma((cols, 2)),
            dma((tops + 1,)),
            dma((2,)),
            dma((2,)),
            dma((cols,)),
            dma((cols,)),
            dma((cols,)),
            dma((cols, rows)),
            dma((2,)),
            dma((2,)),
            dma((tops,)),
            dma((tops,)),
            dma,
            dma((tops,)),
            dma,
            dma((tops, pairs)),
            dma,
            dma((tops,)),
        ],
        compiler_params=pltpu.CompilerParams(
            collective_id=1, has_side_effects=True, vmem_limit_bytes=60 * 2**20
        ),
        name="lower",
    )(
        target[None, :], rhs_in, leaf_inverse, blocks, pattern, rhs, inverse, top_rhs, top_blocks, *rest
    )


def shards(
    rhs_in,
    rhs_target,
    leaf_inverse,
    level_one_blocks,
    level_one_pattern,
    level_one_rhs,
    level_one_inverse,
    top_blocks,
    top_rhs,
    top_inverse,
    top_chain,
):
    leaf_solution, solution_one, top_solution = all_levels(
        rhs_in,
        rhs_target,
        leaf_inverse,
        level_one_blocks[0, 0, 0],
        level_one_pattern[0, 0, 0],
        level_one_rhs[0, 0],
        level_one_inverse[0, 0],
        top_blocks[0, 0],
        top_rhs,
        top_inverse,
        top_chain,
    )
    return (leaf_solution, solution_one[None, None], top_solution)


def solution(mesh):
    in_specs = (
        P(("grid", "row", "col"), None),
        P(("grid", "row", "col")),
        P(("grid", "row", "col"), None, None),
        P("grid", "row", "col", None, None, None, None),
        P("grid", "row", "col", None, None),
        P("grid", "row", None, "col"),
        P("grid", "row", None, None),
        P("grid", "row", None, None, None),
        P(None, None, "col"),
        P(),
        P(),
    )
    out_specs = (
        P(("grid", "row", "col"), None),
        P("grid", "row", None, "col"),
        P(None, None, "col"),
    )
    return jax.shard_map(shards, mesh=mesh, in_specs=in_specs, out_specs=out_specs, check_vma=False)
```

time: 134 us -> 123 us (0.918)
  the two profiles are of different devices: /device:TPU:17 before, /device:TPU:9 now
where the time goes in v1:
time: 123 us; the launch traced here: 121 us
  Pallas kernels  114 us (93%)
  local copies, waits for them, and re-layouts  6.2 us (5%)
    pallas_call x1, Pallas kernels, all_levels(): pl.pallas_call(functools.partial(lower_kernel, sizes, order), out_shape=(...  114 us
    unnamed x7, local copies, waits for them, and re-layouts  4.86 us

profile of v1, /device:TPU:9, one launch (start us, length us, event | category | flops | bytes accessed | tf_op | source)
XLA Modules:
  0.0 121.3 jit_solution(10939640251293552517)
XLA Ops:
  0.6 1.3 %copy.14.pattern_ref = s32[4,2]{1,0:T(4,128)} copy(s32[4,2]{0,1:T(2,128)} %bitcast.13) | data formatting | bytes 64 | tf_op jit(solution)/shard_map/squeeze | solution.py:601
  2.0 114.4 %lower.1 = (bf16[1024,1024]{1,0:T(8,128)(2,1)}, bf16[512,256]{1,0:T(8,128)(2,1)}, bf16[4,512,256]{2,1,0:T(8,128)(2,1)}) custom-call(s32[1,1024]{1,0:T(1,128)} %bitcast.12, bf16[1024,1024]{1,0:T(8,128)(2,1)} %rhs_hbm.1, bf16[2,512,512]{2,1,0:T(8,128)(2,1)} %inverse_hbm.1, bf16[4,2,512,512]{3,2,1,0:T(8,128)(2,1)} %bitcast.7, s32[4,2]{1,0:T(4,128)} %copy.14.pattern_ref, ...), custom_call_target="tpu_custom_call" | custom-call | tf_op jit(solution)/shard_map/lower/pallas_call | solution.py:521
  116.4 0.0 copy-start.1
  116.4 0.0 copy-start
  116.4 3.2 %copy.18 = bf16[1024,1024]{1,0:T(8,128)(2,1)} copy(bf16[1024,1024]{1,0:T(8,128)(2,1)} %get-tuple-element.12) | data formatting | bytes 4194304
  119.6 0.0 copy-done.1
  119.6 0.7 copy.19
  120.3 0.0 copy-done
  120.3 1.0 copy.20
Async XLA Ops:
  116.4 3.2 %copy-start.1 = (bf16[512,256]{1,0:T(8,128)(2,1)S(1)}, bf16[512,256]{1,0:T(8,128)(2,1)}, u32[]{:S(2)}) copy-start(bf16[512,256]{1,0:T(8,128)(2,1)} %get-tuple-element.7) | copy-start | bytes 786436
  116.4 3.9 %copy-start = (bf16[4,512,256]{2,1,0:T(8,128)(2,1)S(1)}, bf16[4,512,256]{2,1,0:T(8,128)(2,1)}, u32[]{:S(2)}) copy-start(bf16[4,512,256]{2,1,0:T(8,128)(2,1)} %get-tuple-element.14) | copy-start | bytes 3145732

commit v2 on v1

--- a/solution.py
+++ b/solution.py
@@ -38,6 +38,33 @@
 
 def dot_t(a, b):
     return lax.dot_general(a, b, (((1,), (1,)), ((), ())), preferred_element_type=jnp.float32)
+
+
+STRIPS = 8
+
+
+def hand_on(leaf_in, one_in, top_in, leaf_out, one_out, top_out, leaf, one, top, sems):
+    moves = []
+    tall = leaf.shape[0] // STRIPS
+    for strip in range(STRIPS):
+        where = pl.ds(strip * tall, tall)
+        moves.append((leaf_in.at[where], leaf.at[where], leaf_out.at[where]))
+    moves += [(one_in, one, one_out), (top_in, top, top_out)]
+    taken = [
+        pltpu.make_async_copy(source, held, sems.at[0, at])
+        for at, (source, held, _) in enumerate(moves)
+    ]
+    given = [
+        pltpu.make_async_copy(held, into, sems.at[1, at])
+        for at, (_, held, into) in enumerate(moves)
+    ]
+    for copy in taken:
+        copy.start()
+    for copy, after in zip(taken, given):
+        copy.wait()
+        after.start()
+    for after in given:
+        after.wait()
 
 
 def lower_kernel(
@@ -122,6 +149,8 @@
     share = got.shape[2]
     group = 128 // share
 
+    units = 2 * cols
+    ahead = 4
     met = greet(("grid", "row", "col"), sizes)
     loads = [
         pltpu.make_async_copy(source, into, load_sems.at[at])
@@ -179,13 +208,13 @@
             device_id_type=MESH,
         )
 
-    def row_copy(part, step):
+    def row_copy(unit, step):
         target = peer(step)
         return pltpu.make_async_remote_copy(
-            src_ref=sorted_rows.at[part, target],
-            dst_ref=got.at[part, me],
-            send_sem=row_send.at[part],
-            recv_sem=row_recv.at[part],
+            src_ref=sorted_rows.at[unit, target],
+            dst_ref=got.at[unit, me],
+            send_sem=row_send.at[unit],
+            recv_sem=row_recv.at[unit],
             device_id=device_of(target),
             device_id_type=MESH,
         )
@@ -199,9 +228,10 @@
         device_id_type=MESH,
     )
 
-    def gather_copy(part, target, owner):
-        return pltpu.make_async_remote_copy(
-            src_ref=solved.at[part, lax.rem(target, 2)],
+    def gather_copy(unit, target, owner):
+        part = unit // 2
+        return pltpu.make_async_remote_copy(
+            src_ref=solved.at[unit],
             dst_ref=gathered.at[part, owner],
             send_sem=gather_send.at[part],
             recv_sem=gather_recv.at[part, owner],
@@ -232,6 +262,14 @@
     rank = jnp.sum(ones * counted, axis=0, keepdims=True).astype(jnp.int32)
     slot = destination * share + rank
 
+    lane = lax.broadcasted_iota(jnp.int32, (128, height), 0)
+    to_lane = jnp.where(lane == lax.rem(me, group) * share + rank, 1.0, 0.0).astype(perm.dtype)
+    high = (ones * (place // 32).astype(jnp.float32)).astype(perm.dtype)
+    low = (ones * lax.rem(place, 32).astype(jnp.float32)).astype(perm.dtype)
+    spread = dot_t(high, to_lane) * 32.0 + dot_t(low, to_lane)
+    places_out[...] = spread.astype(jnp.int32).reshape(devices, 1, 128)
+    got_places[me] = places_out[me]
+
     step_rows = 256
     for begin in range(0, height, step_rows):
         index = lax.broadcasted_iota(jnp.int32, (step_rows, height), 0) + begin
@@ -240,34 +278,29 @@
         )
     loads[1].wait()
 
-    def send_rows(part):
+    def send_rows(unit):
         @pl.loop(1, devices)
         def _(step):
-            row_copy(part, step).start()
+            row_copy(unit, step).start()
 
     for part in range(cols):
         taken = jnp.concatenate([rhs[:, columns(part, which)] for which in range(2)], axis=1)
         moved = dot(perm[...], taken).astype(got.dtype)
-        sorted_rows[part] = moved.reshape(devices, share, chunk)
-        if part == 0:
-            met()
-        if part < 2:
-            send_rows(part)
-        got[part, me] = sorted_rows[part, me]
-        if part == 0:
-            lane = lax.broadcasted_iota(jnp.int32, (128, height), 0)
-            to_lane = jnp.where(lane == lax.rem(me, group) * share + rank, 1.0, 0.0)
-            to_lane = to_lane.astype(perm.dtype)
-            high = (ones * (place // 32).astype(jnp.float32)).astype(perm.dtype)
-            low = (ones * lax.rem(place, 32).astype(jnp.float32)).astype(perm.dtype)
-            spread = dot_t(high, to_lane) * 32.0 + dot_t(low, to_lane)
-            places_out[...] = spread.astype(jnp.int32).reshape(devices, 1, 128)
-
-            @pl.loop(1, devices)
-            def _(step):
-                place_copy(step).start()
-
-            got_places[me] = places_out[me]
+        for which in range(2):
+            unit = 2 * part + which
+            sorted_rows[unit] = moved[:, which * half : (which + 1) * half].reshape(
+                devices, share, half
+            )
+            if unit == 0:
+                met()
+
+                @pl.loop(1, devices)
+                def _(step):
+                    place_copy(step).start()
+
+            if unit < ahead:
+                send_rows(unit)
+            got[unit, me] = sorted_rows[unit, me]
 
     def masked(block, scale):
         return (block.astype(jnp.float32) * scale).astype(block.dtype)
@@ -278,7 +311,7 @@
     def _(owner):
         for leaf_at in range(leaves):
             own_blocks[owner, leaf_at] = masked(
-                own_blocks[owner, leaf_at], pattern_ref[owner, leaf_at].astype(jnp.float32)
+                own_blocks[owner, leaf_at], pattern_ref[leaf_at, owner].astype(jnp.float32)
             )
 
     block_copy.start()
@@ -306,22 +339,31 @@
     for top in range(tops):
         rhs_turned[top] = top_rhs[top].T.reshape(2 * pairs, depth, size)
 
-    def leaf_copy(part, which):
-        return pltpu.make_async_copy(
-            leaf.at[:, columns(part, which)], leaf_hbm.at[:, columns(part, which)], leaf_sems.at[part, which]
-        )
-
-    def solve(part):
-        drain(got.at[part, pl.ds(0, devices - 1)], row_recv.at[part])
-        result = dot(fold[...], got[part].reshape(height, chunk)).astype(leaf.dtype)
-        for which in range(2):
-            solved[part, which] = result[:, which * half : (which + 1) * half]
-        for offset in range(rows - 1, 0, -1):
-            gather_copy(part, row_at(offset), row).start()
-        gathered[part, row] = solved[part, side]
-        for which in range(2):
-            leaf[:, columns(part, which)] = result[:, which * half : (which + 1) * half]
-            leaf_copy(part, which).start()
+    def leaf_copy(unit):
+        where = columns(unit // 2, unit % 2)
+        return pltpu.make_async_copy(leaf.at[:, where], leaf_hbm.at[:, where], leaf_sems.at[unit])
+
+    def solve(unit):
+        part, which = unit // 2, unit % 2
+        drain(got.at[unit, pl.ds(0, devices - 1)], row_recv.at[unit])
+        result = dot(fold[...], got[unit].reshape(height, half)).astype(leaf.dtype)
+        solved[unit] = result
+        for offset in range(1, rows // 2):
+            target = lax.rem(row // 2 + offset, rows // 2) * 2 + which
+            gather_copy(unit, target, row).start()
+
+        @pl.when(side != which)
+        def _():
+            gather_copy(unit, mate, row).start()
+
+        @pl.when(side == which)
+        def _():
+            gathered[part, row] = solved[unit]
+
+        leaf[:, columns(part, which)] = result
+        leaf_copy(unit).start()
+        if unit + ahead < units:
+            send_rows(unit + ahead)
 
     def add(part, owner):
         for which, blocks in enumerate((own_blocks, other_blocks)):
@@ -341,7 +383,7 @@
 
             @pl.when(offset > 0)
             def _():
-                gather_copy(part, owner, owner).wait_recv()
+                gather_copy(2 * part, owner, owner).wait_recv()
 
             add(part, owner)
 
@@ -357,14 +399,12 @@
         def _():
             landed[part % 2, col] = pieces[part, 0]
 
-    for part in range(cols):
-        solve(part)
-        if part + 2 < cols:
-            send_rows(part + 2)
-        if part == 0:
+    for unit in range(units):
+        solve(unit)
+        if unit == 1:
             block_copy.wait()
-        else:
-            couple(part - 1)
+        elif unit > 1 and unit % 2 == 0:
+            couple(unit // 2 - 1)
     couple(cols - 1)
 
     second = 0
@@ -485,11 +525,11 @@
     drain(places_out.at[pl.ds(0, devices - 1)], place_sems.at[0])
     drain(pieces.at[:, 1], piece_send.at[1])
 
+    for unit in range(units):
+        drain(sorted_rows.at[unit, pl.ds(0, devices - 1)], row_send.at[unit])
+        leaf_copy(unit).wait()
     for part in range(cols):
-        drain(sorted_rows.at[part, pl.ds(0, devices - 1)], row_send.at[part])
         drain(gathered.at[part, pl.ds(0, rows - 1)], gather_send.at[part])
-        for which in range(2):
-            leaf_copy(part, which).wait()
     drain(pieces.at[pl.ds(0, cols - 1), 0], piece_send.at[0])
     for top in range(tops):
         mate_copy(top).wait_send()
@@ -518,7 +558,7 @@
     depth = chunk // (2 * pairs)
     held = (rhs_in, leaf_inverse, blocks, rhs, inverse, top_rhs, top_blocks, *rest)
     smem = pl.BlockSpec(memory_space=pltpu.SMEM)
-    return pl.pallas_call(
+    results = pl.pallas_call(
         functools.partial(lower_kernel, sizes, order),
         out_shape=(
             jax.ShapeDtypeStruct((height, width), bf16),
@@ -532,12 +572,12 @@
             *(pltpu.VMEM(array.shape, bf16) for array in held),
             pltpu.VMEM((height, height), bf16),
             pltpu.VMEM((height, height), bf16),
-            pltpu.VMEM((cols, devices, share, chunk), bf16),
-            pltpu.VMEM((cols, devices, share, chunk), bf16),
+            pltpu.VMEM((2 * cols, devices, share, half), bf16),
+            pltpu.VMEM((2 * cols, devices, share, half), bf16),
             pltpu.VMEM((devices, 1, 128), jnp.int32),
             pltpu.VMEM((devices, 1, 128), jnp.int32),
             pltpu.VMEM(blocks.shape, bf16),
-            pltpu.VMEM((cols, 2, height, half), bf16),
+            pltpu.VMEM((2 * cols, height, half), bf16),
             pltpu.VMEM((cols, rows, height, half), bf16),
             pltpu.VMEM((2, size, half), jnp.float32),
             pltpu.VMEM((cols, 2, size, half), bf16),
@@ -552,12 +592,12 @@
             pltpu.VMEM(rhs.shape, bf16),
             pltpu.VMEM(top_rhs.shape, bf16),
             dma((len(held) + 1,)),
-            dma((cols, 2)),
+            dma((2 * cols,)),
             dma((tops + 1,)),
             dma((2,)),
             dma((2,)),
-            dma((cols,)),
-            dma((cols,)),
+            dma((2 * cols,)),
+            dma((2 * cols,)),
             dma((cols,)),
             dma((cols, rows)),
             dma((2,)),
@@ -576,8 +616,19 @@
         ),
         name="lower",
     )(
-        target[None, :], rhs_in, leaf_inverse, blocks, pattern, rhs, inverse, top_rhs, top_blocks, *rest
+        target[None, :], rhs_in, leaf_inverse, blocks, pattern.T, rhs, inverse, top_rhs, top_blocks, *rest
     )
+    return pl.pallas_call(
+        hand_on,
+        out_shape=tuple(jax.ShapeDtypeStruct(result.shape, bf16) for result in results),
+        in_specs=[ANY, ANY, ANY],
+        out_specs=(ANY, ANY, ANY),
+        scratch_shapes=[
+            *(pltpu.VMEM(result.shape, bf16) for result in results),
+            dma((2, STRIPS + 2)),
+        ],
+        name="hand_on",
+    )(*results)
 
 
 def shards(

time: 123 us -> 111 us (0.902); the launches traced: 121 us -> 111 us
  local copies, waits for them, and re-layouts: 6.2 us -> 0 us
  Pallas kernels: 114 us -> 110 us
    pallas_call x1, Pallas kernels: 114 us -> 107 us  [all_levels(): pl.pallas_call(functools.partial(lower_kernel, sizes, order), out_shape=(...]
    unnamed x7 -> x0, local copies, waits for them, and re-layouts: 4.86 us -> none
    pallas_call x0 -> x1, Pallas kernels: none -> 3.23 us  [all_levels(): pl.pallas_call(hand_on, out_shape=tuple((jax.ShapeDtypeStruct(result.shap...]
    squeeze x1 -> x0, local copies, waits for them, and re-layouts: 1.34 us -> none  [shards(): level_one_pattern[0, 0, 0]]
where the time goes in v2:
time: 111 us
  Pallas kernels  110 us (99%)
    pallas_call x1, Pallas kernels, all_levels(): pl.pallas_call(functools.partial(lower_kernel, sizes, order), out_shape=(...  107 us
    pallas_call x1, Pallas kernels, all_levels(): pl.pallas_call(hand_on, out_shape=tuple((jax.ShapeDtypeStruct(result.shap...  3.23 us

profile of v2, /device:TPU:9, one launch (start us, length us, event | category | flops | bytes accessed | tf_op | source)
XLA Modules:
  0.0 111.1 jit_solution(5405016274354332548)
XLA Ops:
  0.6 107.1 %lower.1 = (bf16[1024,1024]{1,0:T(8,128)(2,1)}, bf16[512,256]{1,0:T(8,128)(2,1)}, bf16[4,512,256]{2,1,0:T(8,128)(2,1)}) custom-call(s32[1,1024]{1,0:T(1,128)} %bitcast.13, bf16[1024,1024]{1,0:T(8,128)(2,1)} %rhs_hbm.1, bf16[2,512,512]{2,1,0:T(8,128)(2,1)} %inverse_hbm.1, bf16[4,2,512,512]{3,2,1,0:T(8,128)(2,1)} %bitcast.9, s32[2,4]{1,0:T(2,128)} %bitcast.14, ...), custom_call_target="tpu_custom_call" | custom-call | tf_op jit(solution)/shard_map/lower/pallas_call | solution.py:561
  107.7 3.2 %hand_on.1 = (bf16[1024,1024]{1,0:T(8,128)(2,1)}, bf16[512,256]{1,0:T(8,128)(2,1)}, bf16[4,512,256]{2,1,0:T(8,128)(2,1)}) custom-call(bf16[1024,1024]{1,0:T(8,128)(2,1)} %get-tuple-element.9.leaf_in, bf16[512,256]{1,0:T(8,128)(2,1)} %get-tuple-element.10.one_in, bf16[4,512,256]{2,1,0:T(8,128)(2,1)} %get-tuple-element.11.top_in), custom_call_target="tpu_custom_call" | custom-call | tf_op jit(solution)/shard_map/hand_on/pallas_call | solution.py:621

commit v3 on v2

--- a/solution.py
+++ b/solution.py
@@ -335,9 +335,12 @@
 
     tops = top_blocks.shape[0]
     pairs = grids * rows // 2
-    depth = terms.shape[3]
-    for top in range(tops):
-        rhs_turned[top] = top_rhs[top].T.reshape(2 * pairs, depth, size)
+    splits, depth = terms.shape[0], terms.shape[4]
+    wide = chunk // splits
+    for split in range(splits):
+        for top in range(tops):
+            part_rhs = top_rhs[top, :, split * wide : (split + 1) * wide]
+            rhs_turned[split, top] = part_rhs.T.reshape(2 * pairs, depth, size)
 
     def leaf_copy(unit):
         where = columns(unit // 2, unit % 2)
@@ -411,16 +414,28 @@
     for at in range(1, cols, 2):
         second = second + jnp.where(col == order[at], 1, 0)
     near = side + second - 2 * side * second
-    drain(landed.at[near, pl.ds(0, cols - 1)], piece_recv.at[near])
-    drain(landed.at[1 - near], piece_recv.at[1 - near])
-    update = []
-    for which in range(2):
-        total = landed[which, 0].astype(jnp.float32)
-        for source in range(1, cols):
-            total = total + landed[which, source].astype(jnp.float32)
-        update.append(total)
-    resid = rhs_one[...].astype(jnp.float32) - jnp.concatenate(update, axis=1)
-    solution_one = dot(inverse_one[...], resid.astype(jnp.bfloat16)).astype(one.dtype)
+
+    def level_one(split):
+        update = []
+        for which in range(split * 2 // splits, (split + 1) * 2 // splits):
+
+            @pl.when(near == which)
+            def _(which=which):
+                drain(landed.at[which, pl.ds(0, cols - 1)], piece_recv.at[which])
+
+            @pl.when(near != which)
+            def _(which=which):
+                drain(landed.at[which], piece_recv.at[which])
+
+            total = landed[which, 0].astype(jnp.float32)
+            for source in range(1, cols):
+                total = total + landed[which, source].astype(jnp.float32)
+            update.append(total)
+        where = slice(split * wide, (split + 1) * wide)
+        resid = rhs_one[:, where].astype(jnp.float32) - jnp.concatenate(update, axis=1)
+        solution = dot(inverse_one[...], resid.astype(jnp.bfloat16)).astype(one.dtype)
+        one[:, where] = solution
+        return solution
 
     pair = (lax.axis_index("grid") * rows + row) // 2
     here = 2 * pair + side
@@ -434,93 +449,115 @@
             "row": lax.rem(target, rows // 2) * 2 + side,
         }
 
-    def mate_copy(top):
+    def mate_copy(split, top):
         return pltpu.make_async_remote_copy(
-            src_ref=terms.at[top, 1 - side],
-            dst_ref=mate_terms.at[top],
-            send_sem=mate_send.at[top],
-            recv_sem=mate_recv.at[top],
+            src_ref=terms.at[split, top, 1 - side],
+            dst_ref=mate_terms.at[split, top],
+            send_sem=mate_send.at[split, top],
+            recv_sem=mate_recv.at[split, top],
             device_id={"row": mate},
             device_id_type=MESH,
         )
 
-    def sum_copy(top, target):
+    def sum_copy(split, top, target):
         return pltpu.make_async_remote_copy(
-            src_ref=summed.at[top, target],
-            dst_ref=sums.at[top, pair],
+            src_ref=summed.at[split, top, target],
+            dst_ref=sums.at[split, top, pair],
             send_sem=sum_send,
-            recv_sem=sum_recv.at[top],
+            recv_sem=sum_recv.at[split, top],
             device_id=across(target),
             device_id_type=MESH,
         )
 
-    def out_copy(top, target, source):
+    def out_copy(split, top, target, source):
         return pltpu.make_async_remote_copy(
-            src_ref=stacked.at[top, here],
-            dst_ref=stacked.at[top, 2 * source + side],
+            src_ref=stacked.at[split, top, here],
+            dst_ref=stacked.at[split, top, 2 * source + side],
             send_sem=out_send,
-            recv_sem=out_recv.at[top, source],
+            recv_sem=out_recv.at[split, top, source],
             device_id=across(target),
             device_id_type=MESH,
         )
 
-    def on_copy(top, source):
+    def on_copy(split, top, source):
         return pltpu.make_async_remote_copy(
-            src_ref=stacked.at[top, 2 * source + side],
-            dst_ref=stacked.at[top, 2 * source + side],
+            src_ref=stacked.at[split, top, 2 * source + side],
+            dst_ref=stacked.at[split, top, 2 * source + side],
             send_sem=on_send,
-            recv_sem=on_recv.at[top],
+            recv_sem=on_recv.at[split, top],
             device_id={"row": mate},
             device_id_type=MESH,
         )
 
-    turned = solution_one.T
-    for top in range(tops):
-        term = dot_t(turned, top_blocks[top])
-        for target in range(2 * pairs):
-            terms[top, target % 2, target // 2] = term[
-                target * depth : (target + 1) * depth
-            ].astype(terms.dtype)
-        mate_copy(top).start()
-    one[...] = solution_one
-    one_copy = pltpu.make_async_copy(one, one_hbm, result_sems.at[tops])
-    one_copy.start()
-    for top in range(tops):
-        mate_copy(top).wait_recv()
-        summed[top] = (
-            terms[top, side].astype(jnp.float32) + mate_terms[top].astype(jnp.float32)
-        ).astype(summed.dtype)
-        for step in range(1, pairs):
-            sum_copy(top, pair_at(step)).start()
-    for top in range(tops):
-        sums[top, pair] = summed[top, pair]
-        drain(sums.at[top, pl.ds(0, pairs - 1)], sum_recv.at[top])
-        update = sums[top, 0].astype(jnp.float32)
-        for other in range(1, pairs):
-            update = update + sums[top, other].astype(jnp.float32)
-        running = rhs_turned[top, here].astype(jnp.float32) - update
-        for earlier in range(top):
-            running = running - dot_t(
-                stacked[earlier, here], chain[top * (top - 1) // 2 + earlier]
-            )
-        stacked[top, here] = dot_t(running.astype(jnp.bfloat16), top_inverse[top]).astype(
-            stacked.dtype
-        )
-        for step in range(1, pairs):
-            out_copy(top, pair_at(step), pair).start()
-        on_copy(top, pair).start()
-    top_copies = [
-        pltpu.make_async_copy(top_out.at[top], top_hbm.at[top], result_sems.at[top])
-        for top in range(tops)
-    ]
-    for top in range(tops):
-        for step in range(1, pairs):
-            source = pair_at(step)
-            out_copy(top, source, source).wait_recv()
-            on_copy(top, source).start()
-        drain(stacked.at[top, pl.ds(0, pairs)], on_recv.at[top])
-        top_out[top] = stacked[top].reshape(2 * pairs * depth, size).T
-        top_copies[top].start()
+    def spread_terms(split):
+        turned = level_one(split).T
+        for top in range(tops):
+            term = dot_t(turned, top_blocks[top])
+            for target in range(2 * pairs):
+                terms[split, top, target % 2, target // 2] = term[
+                    target * depth : (target + 1) * depth
+                ].astype(terms.dtype)
+            mate_copy(split, top).start()
+        for top in range(tops):
+            mate_copy(split, top).wait_recv()
+            summed[split, top] = (
+                terms[split, top, side].astype(jnp.float32)
+                + mate_terms[split, top].astype(jnp.float32)
+            ).astype(summed.dtype)
+            for step in range(1, pairs):
+                sum_copy(split, top, pair_at(step)).start()
+            sums[split, top, pair] = summed[split, top, pair]
+
+    def solve_tops(split):
+        for top in range(tops):
+            drain(sums.at[split, top, pl.ds(0, pairs - 1)], sum_recv.at[split, top])
+            update = sums[split, top, 0].astype(jnp.float32)
+            for other in range(1, pairs):
+                update = update + sums[split, top, other].astype(jnp.float32)
+            running = rhs_turned[split, top, here].astype(jnp.float32) - update
+            for earlier in range(top):
+                running = running - dot_t(
+                    stacked[split, earlier, here], chain[top * (top - 1) // 2 + earlier]
+                )
+            stacked[split, top, here] = dot_t(
+                running.astype(jnp.bfloat16), top_inverse[top]
+            ).astype(stacked.dtype)
+            for step in range(1, pairs):
+                out_copy(split, top, pair_at(step), pair).start()
+            on_copy(split, top, pair).start()
+
+    def pass_on(split):
+        for top in range(tops):
+            for step in range(1, pairs):
+                source = pair_at(step)
+                out_copy(split, top, source, source).wait_recv()
+                on_copy(split, top, source).start()
+
+    def top_copy(split, top):
+        where = slice(split * wide, (split + 1) * wide)
+        return pltpu.make_async_copy(
+            top_out.at[top, :, where], top_hbm.at[top, :, where], result_sems.at[split * tops + top]
+        )
+
+    def turn_back(split):
+        for top in range(tops):
+            drain(stacked.at[split, top, pl.ds(0, pairs)], on_recv.at[split, top])
+            turned = stacked[split, top].reshape(2 * pairs * depth, size).T
+            top_out[top, :, split * wide : (split + 1) * wide] = turned
+            top_copy(split, top).start()
+
+    for split in range(splits):
+        spread_terms(split)
+        if split + 1 == splits:
+            one_copy = pltpu.make_async_copy(one, one_hbm, result_sems.at[splits * tops])
+            one_copy.start()
+        if split:
+            pass_on(split - 1)
+        solve_tops(split)
+    for split in range(splits):
+        if split + 1 == splits:
+            pass_on(split)
+        turn_back(split)
 
     drain(places_out.at[pl.ds(0, devices - 1)], place_sems.at[0])
     drain(pieces.at[:, 1], piece_send.at[1])
@@ -531,12 +568,13 @@
     for part in range(cols):
         drain(gathered.at[part, pl.ds(0, rows - 1)], gather_send.at[part])
     drain(pieces.at[pl.ds(0, cols - 1), 0], piece_send.at[0])
-    for top in range(tops):
-        mate_copy(top).wait_send()
-        top_copies[top].wait()
-    drain(summed.at[:, pl.ds(0, pairs - 1)], sum_send)
-    drain(stacked.at[:, pl.ds(0, pairs - 1)], out_send)
-    drain(stacked.at[:, pl.ds(0, pairs)], on_send)
+    for split in range(splits):
+        for top in range(tops):
+            mate_copy(split, top).wait_send()
+            top_copy(split, top).wait()
+    drain(summed.at[:, :, pl.ds(0, pairs - 1)], sum_send)
+    drain(stacked.at[:, :, pl.ds(0, pairs - 1)], out_send)
+    drain(stacked.at[:, :, pl.ds(0, pairs)], on_send)
     one_copy.wait()
 
 
@@ -556,6 +594,8 @@
     tops = top_blocks.shape[0]
     pairs = grids * rows // 2
     depth = chunk // (2 * pairs)
+    splits = 2 if depth % 32 == 0 else 1
+    depth = depth // splits
     held = (rhs_in, leaf_inverse, blocks, rhs, inverse, top_rhs, top_blocks, *rest)
     smem = pl.BlockSpec(memory_space=pltpu.SMEM)
     results = pl.pallas_call(
@@ -582,18 +622,18 @@
             pltpu.VMEM((2, size, half), jnp.float32),
             pltpu.VMEM((cols, 2, size, half), bf16),
             pltpu.VMEM((2, cols, size, half), bf16),
-            pltpu.VMEM((tops, 2 * pairs, depth, size), bf16),
-            pltpu.VMEM((tops, 2, pairs, depth, size), bf16),
-            pltpu.VMEM((tops, pairs, depth, size), bf16),
-            pltpu.VMEM((tops, pairs, depth, size), bf16),
-            pltpu.VMEM((tops, pairs, depth, size), bf16),
-            pltpu.VMEM((tops, 2 * pairs, depth, size), bf16),
+            pltpu.VMEM((splits, tops, 2 * pairs, depth, size), bf16),
+            pltpu.VMEM((splits, tops, 2, pairs, depth, size), bf16),
+            pltpu.VMEM((splits, tops, pairs, depth, size), bf16),
+            pltpu.VMEM((splits, tops, pairs, depth, size), bf16),
+            pltpu.VMEM((splits, tops, pairs, depth, size), bf16),
+            pltpu.VMEM((splits, tops, 2 * pairs, depth, size), bf16),
             pltpu.VMEM((height, width), bf16),
             pltpu.VMEM(rhs.shape, bf16),
             pltpu.VMEM(top_rhs.shape, bf16),
             dma((len(held) + 1,)),
             dma((2 * cols,)),
-            dma((tops + 1,)),
+            dma((splits * tops + 1,)),
             dma((2,)),
             dma((2,)),
             dma((2 * cols,)),
@@ -602,14 +642,14 @@
             dma((cols, rows)),
             dma((2,)),
             dma((2,)),
-            dma((tops,)),
-            dma((tops,)),
+            dma((splits, tops)),
+            dma((splits, tops)),
             dma,
-            dma((tops,)),
+            dma((splits, tops)),
             dma,
-            dma((tops, pairs)),
+            dma((splits, tops, pairs)),
             dma,
-            dma((tops,)),
+            dma((splits, tops)),
         ],
         compiler_params=pltpu.CompilerParams(
             collective_id=1, has_side_effects=True, vmem_limit_bytes=60 * 2**20

time: 111 us -> 108 us (0.973)
  Pallas kernels: 110 us -> 107 us
    pallas_call x1, Pallas kernels: 107 us -> 103 us  [all_levels(): pl.pallas_call(functools.partial(lower_kernel, sizes, order), out_shape=(...]
where the time goes in v3:
time: 108 us; the launch traced here: 107 us
  Pallas kernels  107 us (99%)
    pallas_call x1, Pallas kernels, all_levels(): pl.pallas_call(functools.partial(lower_kernel, sizes, order), out_shape=(...  103 us
    pallas_call x1, Pallas kernels, all_levels(): pl.pallas_call(hand_on, out_shape=tuple((jax.ShapeDtypeStruct(result.shap...  3.23 us

profile of v3, /device:TPU:9, one launch (start us, length us, event | category | flops | bytes accessed | tf_op | source)
XLA Modules:
  0.0 107.4 jit_solution(16098071373945523054)
XLA Ops:
  0.6 103.4 %lower.1 = (bf16[1024,1024]{1,0:T(8,128)(2,1)}, bf16[512,256]{1,0:T(8,128)(2,1)}, bf16[4,512,256]{2,1,0:T(8,128)(2,1)}) custom-call(s32[1,1024]{1,0:T(1,128)} %bitcast.13, bf16[1024,1024]{1,0:T(8,128)(2,1)} %rhs_hbm.1, bf16[2,512,512]{2,1,0:T(8,128)(2,1)} %inverse_hbm.1, bf16[4,2,512,512]{3,2,1,0:T(8,128)(2,1)} %bitcast.9, s32[2,4]{1,0:T(2,128)} %bitcast.14, ...), custom_call_target="tpu_custom_call" | custom-call | tf_op jit(solution)/shard_map/lower/pallas_call | solution.py:601
  104.0 3.2 %hand_on.1 = (bf16[1024,1024]{1,0:T(8,128)(2,1)}, bf16[512,256]{1,0:T(8,128)(2,1)}, bf16[4,512,256]{2,1,0:T(8,128)(2,1)}) custom-call(bf16[1024,1024]{1,0:T(8,128)(2,1)} %get-tuple-element.9.leaf_in, bf16[512,256]{1,0:T(8,128)(2,1)} %get-tuple-element.10.one_in, bf16[4,512,256]{2,1,0:T(8,128)(2,1)} %get-tuple-element.11.top_in), custom_call_target="tpu_custom_call" | custom-call | tf_op jit(solution)/shard_map/hand_on/pallas_call | solution.py:661

commit v4 on v3

--- a/solution.py
+++ b/solution.py
@@ -150,7 +150,7 @@
     group = 128 // share
 
     units = 2 * cols
-    ahead = 4
+    ahead = 2
     met = greet(("grid", "row", "col"), sizes)
     loads = [
         pltpu.make_async_copy(source, into, load_sems.at[at])
@@ -208,13 +208,13 @@
             device_id_type=MESH,
         )
 
-    def row_copy(unit, step):
+    def row_copy(part, step):
         target = peer(step)
         return pltpu.make_async_remote_copy(
-            src_ref=sorted_rows.at[unit, target],
-            dst_ref=got.at[unit, me],
-            send_sem=row_send.at[unit],
-            recv_sem=row_recv.at[unit],
+            src_ref=sorted_rows.at[part, target],
+            dst_ref=got.at[part, me],
+            send_sem=row_send.at[part],
+            recv_sem=row_recv.at[part],
             device_id=device_of(target),
             device_id_type=MESH,
         )
@@ -278,29 +278,25 @@
         )
     loads[1].wait()
 
-    def send_rows(unit):
+    def send_rows(part):
         @pl.loop(1, devices)
         def _(step):
-            row_copy(unit, step).start()
+            row_copy(part, step).start()
 
     for part in range(cols):
         taken = jnp.concatenate([rhs[:, columns(part, which)] for which in range(2)], axis=1)
         moved = dot(perm[...], taken).astype(got.dtype)
-        for which in range(2):
-            unit = 2 * part + which
-            sorted_rows[unit] = moved[:, which * half : (which + 1) * half].reshape(
-                devices, share, half
-            )
-            if unit == 0:
-                met()
-
-                @pl.loop(1, devices)
-                def _(step):
-                    place_copy(step).start()
-
-            if unit < ahead:
-                send_rows(unit)
-            got[unit, me] = sorted_rows[unit, me]
+        sorted_rows[part] = moved.reshape(devices, share, chunk)
+        if part == 0:
+            met()
+
+            @pl.loop(1, devices)
+            def _(step):
+                place_copy(step).start()
+
+        if part < ahead:
+            send_rows(part)
+        got[part, me] = sorted_rows[part, me]
 
     def masked(block, scale):
         return (block.astype(jnp.float32) * scale).astype(block.dtype)
@@ -346,27 +342,26 @@
         where = columns(unit // 2, unit % 2)
         return pltpu.make_async_copy(leaf.at[:, where], leaf_hbm.at[:, where], leaf_sems.at[unit])
 
-    def solve(unit):
-        part, which = unit // 2, unit % 2
-        drain(got.at[unit, pl.ds(0, devices - 1)], row_recv.at[unit])
-        result = dot(fold[...], got[unit].reshape(height, half)).astype(leaf.dtype)
-        solved[unit] = result
-        for offset in range(1, rows // 2):
-            target = lax.rem(row // 2 + offset, rows // 2) * 2 + which
-            gather_copy(unit, target, row).start()
-
-        @pl.when(side != which)
-        def _():
-            gather_copy(unit, mate, row).start()
-
-        @pl.when(side == which)
-        def _():
-            gathered[part, row] = solved[unit]
-
-        leaf[:, columns(part, which)] = result
-        leaf_copy(unit).start()
-        if unit + ahead < units:
-            send_rows(unit + ahead)
+    def solve(part):
+        drain(got.at[part, pl.ds(0, devices - 1)], row_recv.at[part])
+        result = dot(fold[...], got[part].reshape(height, chunk)).astype(leaf.dtype)
+        for which in range(2):
+            unit = 2 * part + which
+            solved[unit] = result[:, which * half : (which + 1) * half]
+            for offset in range(1, rows // 2):
+                target = lax.rem(row // 2 + offset, rows // 2) * 2 + which
+                gather_copy(unit, target, row).start()
+
+            @pl.when(side != which)
+            def _(unit=unit):
+                gather_copy(unit, mate, row).start()
+
+        gathered[part, row] = solved[2 * part + side]
+        if part + ahead < cols:
+            send_rows(part + ahead)
+        for which in range(2):
+            leaf[:, columns(part, which)] = result[:, which * half : (which + 1) * half]
+            leaf_copy(2 * part + which).start()
 
     def add(part, owner):
         for which, blocks in enumerate((own_blocks, other_blocks)):
@@ -402,12 +397,12 @@
         def _():
             landed[part % 2, col] = pieces[part, 0]
 
-    for unit in range(units):
-        solve(unit)
-        if unit == 1:
+    for part in range(cols):
+        solve(part)
+        if part == 0:
             block_copy.wait()
-        elif unit > 1 and unit % 2 == 0:
-            couple(unit // 2 - 1)
+        else:
+            couple(part - 1)
     couple(cols - 1)
 
     second = 0
@@ -526,12 +521,11 @@
                 out_copy(split, top, pair_at(step), pair).start()
             on_copy(split, top, pair).start()
 
-    def pass_on(split):
-        for top in range(tops):
-            for step in range(1, pairs):
-                source = pair_at(step)
-                out_copy(split, top, source, source).wait_recv()
-                on_copy(split, top, source).start()
+    def pass_on(split, top):
+        for step in range(1, pairs):
+            source = pair_at(step)
+            out_copy(split, top, source, source).wait_recv()
+            on_copy(split, top, source).start()
 
     def top_copy(split, top):
         where = slice(split * wide, (split + 1) * wide)
@@ -539,12 +533,11 @@
             top_out.at[top, :, where], top_hbm.at[top, :, where], result_sems.at[split * tops + top]
         )
 
-    def turn_back(split):
-        for top in range(tops):
-            drain(stacked.at[split, top, pl.ds(0, pairs)], on_recv.at[split, top])
-            turned = stacked[split, top].reshape(2 * pairs * depth, size).T
-            top_out[top, :, split * wide : (split + 1) * wide] = turned
-            top_copy(split, top).start()
+    def turn_back(split, top):
+        drain(stacked.at[split, top, pl.ds(0, pairs)], on_recv.at[split, top])
+        turned = stacked[split, top].reshape(2 * pairs * depth, size).T
+        top_out[top, :, split * wide : (split + 1) * wide] = turned
+        top_copy(split, top).start()
 
     for split in range(splits):
         spread_terms(split)
@@ -552,20 +545,27 @@
             one_copy = pltpu.make_async_copy(one, one_hbm, result_sems.at[splits * tops])
             one_copy.start()
         if split:
-            pass_on(split - 1)
+            for top in range(tops):
+                pass_on(split - 1, top)
         solve_tops(split)
-    for split in range(splits):
-        if split + 1 == splits:
-            pass_on(split)
-        turn_back(split)
+    for split in range(splits - 1):
+        for top in range(tops):
+            turn_back(split, top)
+    behind = min(2, tops)
+    for top in range(tops):
+        pass_on(splits - 1, top)
+        if top >= behind:
+            turn_back(splits - 1, top - behind)
+    for top in range(tops - behind, tops):
+        turn_back(splits - 1, top)
 
     drain(places_out.at[pl.ds(0, devices - 1)], place_sems.at[0])
     drain(pieces.at[:, 1], piece_send.at[1])
 
     for unit in range(units):
-        drain(sorted_rows.at[unit, pl.ds(0, devices - 1)], row_send.at[unit])
         leaf_copy(unit).wait()
     for part in range(cols):
+        drain(sorted_rows.at[part, pl.ds(0, devices - 1)], row_send.at[part])
         drain(gathered.at[part, pl.ds(0, rows - 1)], gather_send.at[part])
     drain(pieces.at[pl.ds(0, cols - 1), 0], piece_send.at[0])
     for split in range(splits):
@@ -612,8 +612,8 @@
             *(pltpu.VMEM(array.shape, bf16) for array in held),
             pltpu.VMEM((height, height), bf16),
             pltpu.VMEM((height, height), bf16),
-            pltpu.VMEM((2 * cols, devices, share, half), bf16),
-            pltpu.VMEM((2 * cols, devices, share, half), bf16),
+            pltpu.VMEM((cols, devices, share, chunk), bf16),
+            pltpu.VMEM((cols, devices, share, chunk), bf16),
             pltpu.VMEM((devices, 1, 128), jnp.int32),
             pltpu.VMEM((devices, 1, 128), jnp.int32),
             pltpu.VMEM(blocks.shape, bf16),
@@ -636,8 +636,8 @@
             dma((splits * tops + 1,)),
             dma((2,)),
             dma((2,)),
-            dma((2 * cols,)),
-            dma((2 * cols,)),
+            dma((cols,)),
+            dma((cols,)),
             dma((cols,)),
             dma((cols, rows)),
             dma((2,)),

time: 108 us -> 114 us (1.056)
  Pallas kernels: 107 us -> 112 us
    pallas_call x1, Pallas kernels: 103 us -> 109 us  [all_levels(): pl.pallas_call(functools.partial(lower_kernel, sizes, order), out_shape=(...]
where the time goes in v4:
time: 114 us; the launch traced here: 113 us
  Pallas kernels  112 us (98%)
    pallas_call x1, Pallas kernels, all_levels(): pl.pallas_call(functools.partial(lower_kernel, sizes, order), out_shape=(...  109 us
    pallas_call x1, Pallas kernels, all_levels(): pl.pallas_call(hand_on, out_shape=tuple((jax.ShapeDtypeStruct(result.shap...  3.23 us

profile of v4, /device:TPU:9, one launch (start us, length us, event | category | flops | bytes accessed | tf_op | source)
XLA Modules:
  0.0 112.9 jit_solution(12652074964047761796)
XLA Ops:
  0.6 108.9 %lower.1 = (bf16[1024,1024]{1,0:T(8,128)(2,1)}, bf16[512,256]{1,0:T(8,128)(2,1)}, bf16[4,512,256]{2,1,0:T(8,128)(2,1)}) custom-call(s32[1,1024]{1,0:T(1,128)} %bitcast.13, bf16[1024,1024]{1,0:T(8,128)(2,1)} %rhs_hbm.1, bf16[2,512,512]{2,1,0:T(8,128)(2,1)} %inverse_hbm.1, bf16[4,2,512,512]{3,2,1,0:T(8,128)(2,1)} %bitcast.9, s32[2,4]{1,0:T(2,128)} %bitcast.14, ...), custom_call_target="tpu_custom_call" | custom-call | tf_op jit(solution)/shard_map/lower/pallas_call | solution.py:601
  109.5 3.2 %hand_on.1 = (bf16[1024,1024]{1,0:T(8,128)(2,1)}, bf16[512,256]{1,0:T(8,128)(2,1)}, bf16[4,512,256]{2,1,0:T(8,128)(2,1)}) custom-call(bf16[1024,1024]{1,0:T(8,128)(2,1)} %get-tuple-element.9.leaf_in, bf16[512,256]{1,0:T(8,128)(2,1)} %get-tuple-element.10.one_in, bf16[4,512,256]{2,1,0:T(8,128)(2,1)} %get-tuple-element.11.top_in), custom_call_target="tpu_custom_call" | custom-call | tf_op jit(solution)/shard_map/hand_on/pallas_call | solution.py:661
